TPU v7x, 256 devices: a whole 4x4x8 slice. The times are simulated.
256 devices in a mesh: lon: 8 (over z), lat: 8 (over x, y_hi), dp: 4 (over y_lo, core).
Axes of the slice: x: 4, y: 4 (y_hi: 2, y_lo: 2; y = y_hi * 2 + y_lo), z: 8, core: 2. Of those that a mesh axis runs over, the one named last changes fastest.
Arguments:
- fields: bfloat16 [4, 256, 64, 1024], P('dp', None, 'lat', 'lon'), may hold values from -6 to 6
- weight_one: bfloat16 [9, 256, 256], replicated, may hold values from -0.125 to 0.125
- weight_two: bfloat16 [9, 256, 256], replicated, may hold values from -0.125 to 0.125
- edge_flips: int32 [7, 8], replicated, may hold values from 0 to 1, as said below
- cotangent: bfloat16 [4, 256, 64, 1024], P('dp', None, 'lat', 'lon'), may hold values from -6 to 6
Outputs:
- output: bfloat16 [4, 256, 64, 1024], P('dp', None, 'lat', 'lon')
- grad_fields: bfloat16 [4, 256, 64, 1024], P('dp', None, 'lat', 'lon')
- grad_one: float32 [9, 256, 256], replicated
- grad_two: float32 [9, 256, 256], replicated
Inputs may be any that keep to these rules, and one draw needn't show every extreme that they name: `edge_flips`: 0 on every edge inside a face; only row 8 // 2 - 1, the boundary between the band's two face rows, may hold 1, where the two faces meeting at that longitude tile store longitude in opposite orders.
All inputs are finite; a program needn't handle non-finite values.
Results may differ from a plain program's by a relative error of at most 0.0034.
Values may be sent and summed in bfloat16 or wider, within the bound.
No kernel may reach another device: no remote copies, remote signals or barrier semaphores. Data moves between devices by JAX's collectives and lax.ppermute only.
A program may use at most 128 MiB of HBM per device.

v0:
```python
import jax
import jax.numpy as jnp
from jax import lax
from jax.sharding import PartitionSpec as P


def with_halo(cells, sides, width, closed):
    for axis, dim in sides:
        count = lax.axis_size(axis)
        ends = count if closed else count - 1
        head = lax.slice_in_dim(cells, 0, width, axis=dim)
        tail = lax.slice_in_dim(cells, cells.shape[dim] - width, cells.shape[dim], axis=dim)
        cells = jnp.concatenate(
            [
                lax.ppermute(tail, axis, [(i, (i + 1) % count) for i in range(ends)]),
                cells,
                lax.ppermute(head, axis, [((i + 1) % count, i) for i in range(ends)]),
            ],
            axis=dim,
        )
    return cells


def oriented(line_cells, reverse_flag):
    return jnp.where(reverse_flag == 1, jnp.flip(line_cells, -1), line_cells)


def edge_flags(edge_flips):
    lat_index = lax.axis_index("lat")
    lon_index = lax.axis_index("lon")
    lat_count = lax.axis_size("lat")
    upper_flip = lax.dynamic_slice(edge_flips, (jnp.maximum(lat_index - 1, 0), lon_index), (1, 1))[
        0, 0
    ]
    lower_flip = lax.dynamic_slice(
        edge_flips, (jnp.minimum(lat_index, lat_count - 2), lon_index), (1, 1)
    )[0, 0]
    return (upper_flip, lower_flip, lat_index > 0, lat_index < lat_count - 1)


def padded(source, edge_info):
    upper_flip, lower_flip, has_upper, has_lower = edge_info
    extended = with_halo(source, (("lon", 3), ("lat", 2)), 1, True)
    top_rim = jnp.where(has_upper, extended[:, :, 0, :], jnp.zeros_like(extended[:, :, 0, :]))
    bottom = jnp.where(has_lower, extended[:, :, -1, :], jnp.zeros_like(extended[:, :, -1, :]))
    top_rim = oriented(top_rim, upper_flip)
    bottom = oriented(bottom, lower_flip)
    return jnp.concatenate(
        [top_rim[:, :, None, :], extended[:, :, 1:-1, :], bottom[:, :, None, :]], 2
    )


def patches_of(padded_in, tile_rows, tile_cols):
    return jnp.stack(
        [
            padded_in[:, :, tap_row : tap_row + tile_rows, tap_col : tap_col + tile_cols]
            for tap_row in range(3)
            for tap_col in range(3)
        ],
        1,
    )


def convolve(patches, weight):
    return jnp.einsum("toc,btchw->bohw", weight, patches, preferred_element_type=jnp.float32)


def transposed(grad_tile, weight, tile_rows, tile_cols):
    batch, chans = (grad_tile.shape[0], weight.shape[2])
    padded_grad = jnp.zeros((batch, chans, tile_rows + 2, tile_cols + 2), jnp.float32)
    for tap_row in range(3):
        for tap_col in range(3):
            tap_term = jnp.einsum(
                "oc,bohw->bchw",
                weight[3 * tap_row + tap_col],
                grad_tile,
                preferred_element_type=jnp.float32,
            )
            padded_grad = padded_grad.at[
                :, :, tap_row : tap_row + tile_rows, tap_col : tap_col + tile_cols
            ].add(tap_term)
    return padded_grad


def returned(padded_grad, edge_info):
    upper_flip, lower_flip, has_upper, has_lower = edge_info
    top_rim = oriented(padded_grad[:, :, 0, :], upper_flip)
    bottom = oriented(padded_grad[:, :, -1, :], lower_flip)
    rim_rows = jnp.stack([top_rim, bottom], 2)
    received = with_halo(rim_rows, (("lat", 2),), 1, False)
    interior = padded_grad[:, :, 1:-1, :]
    interior = interior.at[:, :, 0, :].add(received[:, :, 0, :])
    interior = interior.at[:, :, -1, :].add(received[:, :, -1, :])
    side_cols = jnp.stack([interior[..., 0], interior[..., -1]], -1)
    beside = with_halo(side_cols, (("lon", 3),), 1, True)
    result = interior[..., 1:-1]
    result = result.at[..., 0].add(beside[..., 0])
    result = result.at[..., -1].add(beside[..., -1])
    return result


def per_device(fields, weight_one, weight_two, edge_flips, cotangent):
    tile_rows, tile_cols = (fields.shape[2], fields.shape[3])
    edge_info = edge_flags(edge_flips)
    patch_in = patches_of(padded(fields, edge_info), tile_rows, tile_cols)
    hidden = convolve(patch_in, weight_one)
    activation = jax.nn.silu(hidden).astype(jnp.bfloat16)
    patch_act = patches_of(padded(activation, edge_info), tile_rows, tile_cols)
    output = (fields.astype(jnp.float32) + convolve(patch_act, weight_two)).astype(jnp.bfloat16)
    local_two = jnp.einsum(
        "bohw,btchw->toc", cotangent, patch_act, preferred_element_type=jnp.float32
    )
    back_act = returned(transposed(cotangent, weight_two, tile_rows, tile_cols), edge_info)
    sigmoid_h = jax.nn.sigmoid(hidden)
    back_hidden = (back_act * sigmoid_h * (1.0 + hidden * (1.0 - sigmoid_h))).astype(jnp.bfloat16)
    local_one = jnp.einsum(
        "bohw,btchw->toc", back_hidden, patch_in, preferred_element_type=jnp.float32
    )
    grad_one, grad_two = lax.psum((local_one, local_two), ("lon", "lat", "dp"))
    back_fields = returned(transposed(back_hidden, weight_one, tile_rows, tile_cols), edge_info)
    grad_fields = (cotangent.astype(jnp.float32) + back_fields).astype(jnp.bfloat16)
    return (output, grad_fields, grad_one, grad_two)


def solution(mesh):
    in_specs = (P("dp", None, "lat", "lon"), P(), P(), P(), P("dp", None, "lat", "lon"))
    out_specs = (P("dp", None, "lat", "lon"), P("dp", None, "lat", "lon"), P(), P())
    return jax.shard_map(
        per_device, mesh=mesh, in_specs=in_specs, out_specs=out_specs, check_vma=False
    )
```

profile of v0, /device:TPU:97, one launch (start us, length us, event | category | flops | bytes accessed | tf_op | source)
XLA Modules:
  0.0 453.6 jit_solution(17974031605681476931)
XLA Ops:
  7.2 1.4 copy.9
  8.6 2.9 collective-permute-start
  12.8 1.4 and_reduce_fusion
  14.2 1.2 convolution_bitcast_fusion.17
  15.6 2.5 fusion.20
  18.1 4.0 scatter-add.89
  22.1 3.2 add_select_fusion.1
  25.3 4.0 scatter-add.90
  29.3 1.3 fusion.22
  30.6 1.3 fusion.23
  31.9 2.7 scatter-add.94
  34.6 1.3 fusion.24
  35.9 2.7 scatter-add.95
  38.6 1.3 fusion.26
  39.9 1.3 fusion.27
  41.1 2.7 scatter-add.99
  43.9 1.2 fusion.28
  45.1 2.7 scatter-add.100
  47.9 1.4 fusion.131
  51.2 5.2 %collective-permute-start.3 = (bf16[1,256,1,130]{1,3,2,0:T(8,128)(2,1)S(1)}, bf16[1,256,1,130]{1,3,2,0:T(8,128)(2,1)S(1)}, u32[]{:S(2)}, u32[]{:S(2)}) collective-permute-start(bf16[1,256,1,130]{1,3,2,0:T(8,128)(2,1)S(1)} %get-tuple-element.342), channel_id=1, source_target_pairs={{4,0},{8,4},{12,8},{16,12},{20,16},{24,20},{28,24},{0,28},{5,1},{9... | collective-permute-start | bytes 199688 | tf_op jit(solution)/shard_map/ppermute | solution.py:17
  56.5 1.3 collective-permute-start.9
  57.8 5.5 %collective-permute-start.8 = (f32[1,256,1,130]{1,3,2,0:T(8,128)S(1)}, f32[1,256,1,130]{1,3,2,0:T(8,128)S(1)}, u32[]{:S(2)}, u32[]{:S(2)}) collective-permute-start(f32[1,256,1,130]{1,3,2,0:T(8,128)S(1)} %get-tuple-element.327), channel_id=1, source_target_pairs={{0,4},{4,8},{8,12},{12,16},{16,20},{20,24},{24,28},{1,5},{5,9},{9,... | collective-permute-start | bytes 399368 | tf_op jit(solution)/shard_map/ppermute | solution.py:15
  63.3 1.1 slice.1095
  64.7 6.4 %collective-permute-done.2 = bf16[1,256,1,130]{1,3,2,0:T(8,128)(2,1)S(1)} collective-permute-done((bf16[1,256,1,130]{1,3,2,0:T(8,128)(2,1)S(1)}, bf16[1,256,1,130]{1,3,2,0:T(8,128)(2,1)S(1)}, u32[]{:S(2)}, u32[]{:S(2)}) %collective-permute-start.2) | collective-permute-done | bytes 66592 | tf_op jit(solution)/shard_map/ppermute | solution.py:15
  72.6 0.9 copy-done.1
  73.6 2.7 collective-permute-start.10
  76.4 2.1 copy-done.8
  78.6 1.1 slice.1100
  79.7 1.5 scatter-add.105
  81.2 2.2 collective-permute-done.11
  84.2 1.5 scatter-add.106
  85.7 4.4 multiply_convert_fusion
  90.1 2.9 fusion.8
  93.3 2.6 fusion.29
  96.6 1.0 collective-permute-start.5
  97.6 7.2 %scatter-add.110 = f32[1,256,10,130]{1,3,2,0:T(8,128)S(1)} dynamic-update-slice(f32[1,256,10,130]{1,3,2,0:T(8,128)S(1)} %scatter-add.109, f32[1,256,8,128]{1,3,2,0:T(8,128)} %fusion.29, s32[]{:T(128)} %constant.657.clone.1, s32[]{:T(128)} %constant.657.clone.1, s32[]{:T(128)} %bitcast.51, s32[]{:T(128)} %bitcast.52) | dynamic-update-slice | bytes 2097156 | tf_op jit(solution)/shard_map/scatter-add | solution.py:81
  104.8 4.1 add_select_fusion
  108.9 7.2 %scatter-add.111 = f32[1,256,10,130]{1,3,2,0:T(8,128)S(1)} dynamic-update-slice(f32[1,256,10,130]{1,3,2,0:T(8,128)S(1)} %scatter-add.110, f32[1,256,8,128]{1,3,2,0:T(8,128)} %add_select_fusion, s32[]{:T(128)} %constant.657.clone.1, s32[]{:T(128)} %constant.657.clone.1, s32[]{:T(128)} %bitcast.57, s32[]{:T(128)} %bitcast.58) | dynamic-update-slice | bytes 2097156 | tf_op jit(solution)/shard_map/scatter-add | solution.py:81
  116.1 1.2 fusion.31
  117.3 2.2 fusion.32
  119.5 5.9 %scatter-add.115 = f32[1,256,10,130]{1,3,2,0:T(8,128)S(1)} dynamic-update-slice(f32[1,256,10,130]{1,3,2,0:T(8,128)S(1)} %fusion.31, f32[1,256,8,128]{1,3,2,0:T(8,128)} %fusion.32, s32[]{:T(128)} %constant.657.clone.1, s32[]{:T(128)} %constant.657.clone.1, s32[]{:T(128)} %constant.670.clone.1, s32[]{:T(128)} %constant.670.clone.1) | dynamic-update-slice | bytes 2097156 | tf_op jit(solution)/shard_map/scatter-add | solution.py:81
  125.4 2.2 fusion.33
  127.6 5.9 %scatter-add.116 = f32[1,256,10,130]{1,3,2,0:T(8,128)S(1)} dynamic-update-slice(f32[1,256,10,130]{1,3,2,0:T(8,128)S(1)} %scatter-add.115, f32[1,256,8,128]{1,3,2,0:T(8,128)} %fusion.33, s32[]{:T(128)} %constant.657.clone.1, s32[]{:T(128)} %constant.657.clone.1, s32[]{:T(128)} %constant.670.clone.1, s32[]{:T(128)} %constant.667.clone.1) | dynamic-update-slice | bytes 2097156 | tf_op jit(solution)/shard_map/scatter-add | solution.py:81
  133.4 1.2 fusion.35
  134.6 2.2 fusion.36
  136.8 5.9 %scatter-add.120 = f32[1,256,10,130]{1,3,2,0:T(8,128)S(1)} dynamic-update-slice(f32[1,256,10,130]{1,3,2,0:T(8,128)S(1)} %fusion.35, f32[1,256,8,128]{1,3,2,0:T(8,128)} %fusion.36, s32[]{:T(128)} %constant.657.clone.1, s32[]{:T(128)} %constant.657.clone.1, s32[]{:T(128)} %constant.667.clone.1, s32[]{:T(128)} %constant.670.clone.1) | dynamic-update-slice | bytes 2097156 | tf_op jit(solution)/shard_map/scatter-add | solution.py:81
  143.4 2.2 fusion.37
  145.6 5.9 %scatter-add.121 = f32[1,256,10,130]{1,3,2,0:T(8,128)S(1)} dynamic-update-slice(f32[1,256,10,130]{1,3,2,0:T(8,128)S(1)} %scatter-add.120, f32[1,256,8,128]{1,3,2,0:T(8,128)} %fusion.37, s32[]{:T(128)} %constant.657.clone.1, s32[]{:T(128)} %constant.657.clone.1, s32[]{:T(128)} %constant.667.clone.1, s32[]{:T(128)} %constant.667.clone.1) | dynamic-update-slice | bytes 2097156 | tf_op jit(solution)/shard_map/scatter-add | solution.py:81
  151.5 3.0 collective-permute-start.6
  155.7 2.6 collective-permute-done.6
  160.8 2.1 copy-done.10
  162.9 2.9 fusion.11
  166.5 3.0 collective-permute-start.12
  169.9 1.4 collective-permute-start.13
  171.4 6.0 %collective-permute-done.13 = f32[1,256,1,130]{1,3,2,0:T(8,128)S(1)} collective-permute-done((f32[1,256,1,130]{1,3,2,0:T(8,128)S(1)}, f32[1,256,1,130]{1,3,2,0:T(8,128)S(1)}, u32[]{:S(2)}, u32[]{:S(2)}) %collective-permute-start.13) | collective-permute-done | bytes 133152 | tf_op jit(solution)/shard_map/ppermute | solution.py:17
  177.4 1.0 copy-done.2
  178.4 1.8 collective-permute-start.14
  180.2 3.8 fusion.41
  184.0 1.1 copy.36
  185.4 3.6 collective-permute-done.15
  189.2 1.1 copy.37
  190.3 251.3 %all-reduce.5.cloned.1.call-done = (f32[9,256,256]{1,2,0:T(8,128)}, f32[9,256,256]{1,2,0:T(8,128)}) async-done(((f32[9,256,256]{1,2,0:T(8,128)}, f32[9,256,256]{1,2,0:T(8,128)}), (f32[9,256,256]{1,2,0:T(8,128)}, f32[9,256,256]{1,2,0:T(8,128)})) %all-reduce.5.cloned.1.call-update) | async-done | bytes 4718608 | tf_op jit(solution)/shard_map/psum | solution.py:119
  441.6 3.2 copy.38
  444.8 1.9 copy.39
  (104 shorter events, 11.8 us)
Async XLA Ops:
  7.2 7.0 %copy-start = (bf16[1,256,8,128]{3,2,1,0:T(8,128)(2,1)S(1)}, bf16[1,256,8,128]{3,2,1,0:T(8,128)(2,1)}, u32[]{:S(2)}) copy-start(bf16[1,256,8,128]{3,2,1,0:T(8,128)(2,1)} %param.61) | copy-start | bytes 1572868
  7.2 434.4 %all-reduce.5.cloned.1.call-start = ((), (), s32[]{:S(2)}) async-start(), calls=%async_computation | async-start | bytes 9437184 | tf_op jit(solution)/shard_map/psum | solution.py:119
  8.6 42.5 %collective-permute-start = (bf16[1,256,8,1]{1,3,2,0:T(2,128)(2,1)S(1)}, bf16[1,256,8,1]{1,3,2,0:T(2,128)(2,1)S(1)}, u32[]{:S(2)}, u32[]{:S(2)}) collective-permute-start(bf16[1,256,8,1]{1,3,2,0:T(2,128)(2,1)S(1)} %get-tuple-element.346), channel_id=1, source_target_pairs={{0,32},{32,64},{64,96},{96,128},{128,160},{160,192},{192,224},{224... | collective-permute-start | bytes 12296 | tf_op jit(solution)/shard_map/ppermute | solution.py:15
  11.5 39.6 %collective-permute-start.1 = (bf16[1,256,8,1]{1,3,2,0:T(2,128)(2,1)S(1)}, bf16[1,256,8,1]{1,3,2,0:T(2,128)(2,1)S(1)}, u32[]{:S(2)}, u32[]{:S(2)}) collective-permute-start(bf16[1,256,8,1]{1,3,2,0:T(2,128)(2,1)S(1)} %get-tuple-element.347), channel_id=1, source_target_pairs={{32,0},{64,32},{96,64},{128,96},{160,128},{192,160},{224,192},{0,2... | collective-permute-start | bytes 12296 | tf_op jit(solution)/shard_map/ppermute | solution.py:17
  51.2 13.1 %collective-permute-start.3 = (bf16[1,256,1,130]{1,3,2,0:T(8,128)(2,1)S(1)}, bf16[1,256,1,130]{1,3,2,0:T(8,128)(2,1)S(1)}, u32[]{:S(2)}, u32[]{:S(2)}) collective-permute-start(bf16[1,256,1,130]{1,3,2,0:T(8,128)(2,1)S(1)} %get-tuple-element.342), channel_id=1, source_target_pairs={{4,0},{8,4},{12,8},{16,12},{20,16},{24,20},{28,24},{0,28},{5,1},{9... | collective-permute-start | bytes 199688 | tf_op jit(solution)/shard_map/ppermute | solution.py:17
  56.5 17.0 %collective-permute-start.9 = (f32[1,256,1,130]{1,3,2,0:T(8,128)S(1)}, f32[1,256,1,130]{1,3,2,0:T(8,128)S(1)}, u32[]{:S(2)}, u32[]{:S(2)}) collective-permute-start(f32[1,256,1,130]{1,3,2,0:T(8,128)S(1)} %get-tuple-element.326), channel_id=1, source_target_pairs={{4,0},{8,4},{12,8},{16,12},{20,16},{24,20},{28,24},{5,1},{9,5},{13... | collective-permute-start | bytes 399368 | tf_op jit(solution)/shard_map/ppermute | solution.py:17
  57.8 14.8 %collective-permute-start.8 = (f32[1,256,1,130]{1,3,2,0:T(8,128)S(1)}, f32[1,256,1,130]{1,3,2,0:T(8,128)S(1)}, u32[]{:S(2)}, u32[]{:S(2)}) collective-permute-start(f32[1,256,1,130]{1,3,2,0:T(8,128)S(1)} %get-tuple-element.327), channel_id=1, source_target_pairs={{0,4},{4,8},{8,12},{12,16},{16,20},{20,24},{24,28},{1,5},{5,9},{9,... | collective-permute-start | bytes 399368 | tf_op jit(solution)/shard_map/ppermute | solution.py:15
  64.3 6.8 %collective-permute-start.2 = (bf16[1,256,1,130]{1,3,2,0:T(8,128)(2,1)S(1)}, bf16[1,256,1,130]{1,3,2,0:T(8,128)(2,1)S(1)}, u32[]{:S(2)}, u32[]{:S(2)}) collective-permute-start(bf16[1,256,1,130]{1,3,2,0:T(8,128)(2,1)S(1)} %get-tuple-element.343), channel_id=1, source_target_pairs={{0,4},{4,8},{8,12},{12,16},{16,20},{20,24},{24,28},{28,0},{1,5},{5... | collective-permute-start | bytes 199688 | tf_op jit(solution)/shard_map/ppermute | solution.py:15
  72.2 1.3 copy-start.1
  73.6 12.2 %copy-start.5 = (bf16[9,256,256]{2,1,0:T(8,128)(2,1)S(1)}, bf16[9,256,256]{2,1,0:T(8,128)(2,1)}, u32[]{:S(2)}) copy-start(bf16[9,256,256]{2,1,0:T(8,128)(2,1)} %param.58) | copy-start | bytes 3538948
  73.6 6.1 %collective-permute-start.10 = (f32[1,256,8,1]{1,3,2,0:T(1,128)S(1)}, f32[1,256,8,1]{1,3,2,0:T(1,128)S(1)}, u32[]{:S(2)}, u32[]{:S(2)}) collective-permute-start(f32[1,256,8,1]{1,3,2,0:T(1,128)S(1)} %get-tuple-element.333), channel_id=1, source_target_pairs={{0,32},{32,64},{64,96},{96,128},{128,160},{160,192},{192,224},{224... | collective-permute-start | bytes 24584 | tf_op jit(solution)/shard_map/ppermute | solution.py:15
  76.4 2.1 copy-start.8
  79.7 3.7 collective-permute-start.11
  85.7 4.4 copy-start.9
  96.0 46.7 %collective-permute-start.4 = (bf16[1,256,8,1]{1,3,2,0:T(2,128)(2,1)S(1)}, bf16[1,256,8,1]{1,3,2,0:T(2,128)(2,1)S(1)}, u32[]{:S(2)}, u32[]{:S(2)}) collective-permute-start(bf16[1,256,8,1]{1,3,2,0:T(2,128)(2,1)S(1)} %get-tuple-element.344), channel_id=1, source_target_pairs={{0,32},{32,64},{64,96},{96,128},{128,160},{160,192},{192,224},{224... | collective-permute-start | bytes 12296 | tf_op jit(solution)/shard_map/ppermute | solution.py:15
  96.6 46.1 %collective-permute-start.5 = (bf16[1,256,8,1]{1,3,2,0:T(2,128)(2,1)S(1)}, bf16[1,256,8,1]{1,3,2,0:T(2,128)(2,1)S(1)}, u32[]{:S(2)}, u32[]{:S(2)}) collective-permute-start(bf16[1,256,8,1]{1,3,2,0:T(2,128)(2,1)S(1)} %get-tuple-element.345), channel_id=1, source_target_pairs={{32,0},{64,32},{96,64},{128,96},{160,128},{192,160},{224,192},{0,2... | collective-permute-start | bytes 12296 | tf_op jit(solution)/shard_map/ppermute | solution.py:17
  143.4 11.1 %collective-permute-start.7 = (bf16[1,256,1,130]{1,3,2,0:T(8,128)(2,1)}, bf16[1,256,1,130]{1,3,2,0:T(8,128)(2,1)}, u32[]{:S(2)}, u32[]{:S(2)}) collective-permute-start(bf16[1,256,1,130]{1,3,2,0:T(8,128)(2,1)} %get-tuple-element.338), channel_id=1, source_target_pairs={{4,0},{8,4},{12,8},{16,12},{20,16},{24,20},{28,24},{0,28},{5,1},{9... | collective-permute-start | bytes 199688 | tf_op jit(solution)/shard_map/ppermute | solution.py:17
  145.6 5.9 %copy-start.7 = (bf16[1,256,1,130]{1,3,2,0:T(8,128)(2,1)S(1)}, bf16[1,256,1,130]{1,3,2,0:T(8,128)(2,1)}, u32[]{:S(2)}) copy-start(bf16[1,256,1,130]{1,3,2,0:T(8,128)(2,1)} %get-tuple-element.339) | copy-start | bytes 199684
  151.5 6.9 %collective-permute-start.6 = (bf16[1,256,1,130]{1,3,2,0:T(8,128)(2,1)S(1)}, bf16[1,256,1,130]{1,3,2,0:T(8,128)(2,1)S(1)}, u32[]{:S(2)}, u32[]{:S(2)}) collective-permute-start(bf16[1,256,1,130]{1,3,2,0:T(8,128)(2,1)S(1)} %copy-done.7), channel_id=1, source_target_pairs={{0,4},{4,8},{8,12},{12,16},{16,20},{20,24},{24,28},{28,0},{1,5},{5... | collective-permute-start | bytes 199688 | tf_op jit(solution)/shard_map/ppermute | solution.py:15
  160.8 2.1 copy-start.10
  166.5 4.9 %collective-permute-start.12 = (f32[1,256,1,130]{1,3,2,0:T(8,128)S(1)}, f32[1,256,1,130]{1,3,2,0:T(8,128)S(1)}, u32[]{:S(2)}, u32[]{:S(2)}) collective-permute-start(f32[1,256,1,130]{1,3,2,0:T(8,128)S(1)} %get-tuple-element.323), channel_id=1, source_target_pairs={{0,4},{4,8},{8,12},{12,16},{16,20},{20,24},{24,28},{1,5},{5,9},{9,... | collective-permute-start | bytes 399368 | tf_op jit(solution)/shard_map/ppermute | solution.py:15
  169.8 10.4 %copy-start.6 = (bf16[9,256,256]{2,1,0:T(8,128)(2,1)S(1)}, bf16[9,256,256]{2,1,0:T(8,128)(2,1)}, u32[]{:S(2)}) copy-start(bf16[9,256,256]{2,1,0:T(8,128)(2,1)} %param.59) | copy-start | bytes 3538948
  169.9 7.4 %collective-permute-start.13 = (f32[1,256,1,130]{1,3,2,0:T(8,128)S(1)}, f32[1,256,1,130]{1,3,2,0:T(8,128)S(1)}, u32[]{:S(2)}, u32[]{:S(2)}) collective-permute-start(f32[1,256,1,130]{1,3,2,0:T(8,128)S(1)} %get-tuple-element.322), channel_id=1, source_target_pairs={{4,0},{8,4},{12,8},{16,12},{20,16},{24,20},{28,24},{5,1},{9,5},{13... | collective-permute-start | bytes 399368 | tf_op jit(solution)/shard_map/ppermute | solution.py:17
  177.4 1.0 copy-start.2
  178.4 6.9 %collective-permute-start.14 = (f32[1,256,8,1]{1,3,2,0:T(1,128)S(1)}, f32[1,256,8,1]{1,3,2,0:T(1,128)S(1)}, u32[]{:S(2)}, u32[]{:S(2)}) collective-permute-start(f32[1,256,8,1]{1,3,2,0:T(1,128)S(1)} %get-tuple-element.331), channel_id=1, source_target_pairs={{0,32},{32,64},{64,96},{96,128},{128,160},{160,192},{192,224},{224... | collective-permute-start | bytes 24584 | tf_op jit(solution)/shard_map/ppermute | solution.py:15
  180.2 4.9 %copy-start.3 = (f32[1,256,8,130]{1,3,2,0:T(8,128)S(1)}, f32[1,256,8,130]{1,3,2,0:T(8,128)}, u32[]{:S(2)}) copy-start(f32[1,256,8,130]{1,3,2,0:T(8,128)} %copy-done.2) | copy-start | bytes 3194884
  185.2 3.8 collective-permute-start.15
  441.6 3.2 copy-start.4
Sparse Core Ops, SparseCore 0:
  165.9 275.6 all-reduce.4
where the time goes:
time: 455 us; the launch traced here: 454 us
  waiting for transfers between devices  272 us (60%)
  local copies, waits for them, and re-layouts  84.1 us (18%)
  matrix products  46.6 us (10%)
  starting transfers between devices  28.6 us (6%)
  between operations  16.1 us (4%)
  other arithmetic  6.15 us (1%)
    psum x1, waiting for transfers between devices, per_device(): grad_one, grad_two = lax.psum((local_one, local_two), ('lon', 'lat', 'dp'))  251 us
    scatter-add x14, local copies, waits for them, and re-layouts, transposed(): padded_grad = padded_grad.at[:, :, tap_row:tap_row + tile_rows, tap_col:t...  57 us
    dot_general x18, matrix products, transposed(): jnp.einsum('oc,bohw->bchw', weight[3 * tap_row + tap_col], grad_tile, pre...  32.6 us
    ppermute x8, starting transfers between devices, with_halo(): lax.ppermute(tail, axis, [(i, (i + 1) % count) for i in range(ends)])  19.6 us
    unnamed x40, local copies, waits for them, and re-layouts  16.1 us
    ppermute x8, waiting for transfers between devices, with_halo(): lax.ppermute(head, axis, [((i + 1) % count, i) for i in range(ends)])  11.8 us
  transfers between devices with their start and end apart: 17, of which 6 were waited for; matrix products, arithmetic and copies ran while one was open for 23% of the time, Pallas kernels for 0%

commit v1 on v0

--- a/solution.py
+++ b/solution.py
@@ -116,7 +116,7 @@
     local_one = jnp.einsum(
         "bohw,btchw->toc", back_hidden, patch_in, preferred_element_type=jnp.float32
     )
-    grad_one, grad_two = lax.psum((local_one, local_two), ("lon", "lat", "dp"))
+    grad_one, grad_two = lax.psum(lax.psum((local_one, local_two), ("lat", "dp")), "lon")
     back_fields = returned(transposed(back_hidden, weight_one, tile_rows, tile_cols), edge_info)
     grad_fields = (cotangent.astype(jnp.float32) + back_fields).astype(jnp.bfloat16)
     return (output, grad_fields, grad_one, grad_two)

time: 455 us -> 379 us (0.83)
  waiting for transfers between devices: 272 us -> 180 us
  other arithmetic: 6.15 us -> 11.4 us
    psum x1 -> x2, waiting for transfers between devices: 251 us -> 155 us  [the longest x1 120 us: per_device(): lax.psum((local_one, local_two), ('lat', 'dp'))]
    rev x8, local copies, waits for them, and re-layouts: 2.56 us -> 7.26 us  [oriented(): return jnp.where(reverse_flag == 1, jnp.flip(line_cells, -1), line_cells)]
    unnamed x40 -> x44, local copies, waits for them, and re-layouts: 16.1 us -> 16.6 us
  transfers between devices with their start and end apart: 17 -> 18, of which waited for: 6 -> 10; matrix products, arithmetic and copies ran while one was open for 23% -> 32% of each run, Pallas kernels for 0% -> 0%
where the time goes in v1:
time: 379 us; the launch traced here: 375 us
  waiting for transfers between devices  180 us (47%)
  local copies, waits for them, and re-layouts  87.7 us (23%)
  matrix products  48.9 us (13%)
  starting transfers between devices  31.2 us (8%)
  between operations  16.1 us (4%)
  other arithmetic  11.4 us (3%)
    psum x1, waiting for transfers between devices, per_device(): lax.psum((local_one, local_two), ('lat', 'dp'))  120 us
    scatter-add x14, local copies, waits for them, and re-layouts, transposed(): padded_grad = padded_grad.at[:, :, tap_row:tap_row + tile_rows, tap_col:t...  56.5 us
    psum x1, waiting for transfers between devices, per_device(): lax.psum(lax.psum((local_one, local_two), ('lat', 'dp')), 'lon')  35.3 us
    dot_general x18, matrix products, transposed(): jnp.einsum('oc,bohw->bchw', weight[3 * tap_row + tap_col], grad_tile, pre...  34.4 us
    ppermute x8, starting transfers between devices, with_halo(): lax.ppermute(tail, axis, [(i, (i + 1) % count) for i in range(ends)])  20 us
    unnamed x44, local copies, waits for them, and re-layouts  16.6 us
    ppermute x8, waiting for transfers between devices, with_halo(): lax.ppermute(head, axis, [((i + 1) % count, i) for i in range(ends)])  14 us
    ppermute x8, starting transfers between devices, with_halo(): lax.ppermute(head, axis, [((i + 1) % count, i) for i in range(ends)])  11.2 us
  transfers between devices with their start and end apart: 18, of which 10 were waited for; matrix products, arithmetic and copies ran while one was open for 32% of the time, Pallas kernels for 0%

profile of v1, /device:TPU:97, one launch (start us, length us, event | category | flops | bytes accessed | tf_op | source)
XLA Modules:
  0.0 375.1 jit_solution(8747877026842868022)
XLA Ops:
  7.2 1.4 copy.9
  8.6 2.9 collective-permute-start
  12.7 1.4 and_reduce_fusion
  14.1 1.2 convolution_bitcast_fusion.17
  15.5 2.4 fusion.20
  17.9 3.8 %scatter-add.89 = f32[1,256,10,130]{1,3,2,0:T(8,128)S(1)} dynamic-update-slice(f32[1,256,10,130]{1,3,2,0:T(8,128)S(1)} %scatter-add.86, f32[1,256,8,128]{1,3,2,0:T(8,128)S(1)} %fusion.20, s32[]{:T(128)} %constant.657.clone.1, s32[]{:T(128)} %constant.657.clone.1, s32[]{:T(128)} %bitcast.51, s32[]{:T(128)} %bitcast.52) | dynamic-update-slice | bytes 2097156 | tf_op jit(solution)/shard_map/scatter-add | solution.py:81
  21.7 3.1 add_select_fusion.1
  24.8 4.0 %scatter-add.90 = f32[1,256,10,130]{1,3,2,0:T(8,128)S(1)} dynamic-update-slice(f32[1,256,10,130]{1,3,2,0:T(8,128)S(1)} %scatter-add.89, f32[1,256,8,128]{1,3,2,0:T(8,128)S(1)} %add_select_fusion.1, s32[]{:T(128)} %constant.657.clone.1, s32[]{:T(128)} %constant.657.clone.1, s32[]{:T(128)} %bitcast.57, s32[]{:T(128)} %bitcast.58) | dynamic-update-slice | bytes 2097156 | tf_op jit(solution)/shard_map/scatter-add | solution.py:81
  28.8 1.3 fusion.22
  30.1 1.3 fusion.23
  31.3 2.7 scatter-add.94
  34.0 1.3 fusion.24
  35.3 2.7 scatter-add.95
  38.0 1.3 fusion.26
  39.3 1.3 fusion.27
  40.6 2.7 scatter-add.99
  43.3 1.3 fusion.28
  44.6 2.7 scatter-add.100
  47.3 1.4 fusion.131
  51.3 5.1 %collective-permute-start.3 = (bf16[1,256,1,130]{1,3,2,0:T(8,128)(2,1)}, bf16[1,256,1,130]{1,3,2,0:T(8,128)(2,1)}, u32[]{:S(2)}, u32[]{:S(2)}) collective-permute-start(bf16[1,256,1,130]{1,3,2,0:T(8,128)(2,1)} %get-tuple-element.344), channel_id=1, source_target_pairs={{4,0},{8,4},{12,8},{16,12},{20,16},{24,20},{28,24},{0,28},{5,1},{9... | collective-permute-start | bytes 199688 | tf_op jit(solution)/shard_map/ppermute | solution.py:17
  57.2 1.3 collective-permute-start.9
  58.5 6.2 %collective-permute-start.8 = (f32[1,256,1,130]{1,3,2,0:T(8,128)}, f32[1,256,1,130]{1,3,2,0:T(8,128)}, u32[]{:S(2)}, u32[]{:S(2)}) collective-permute-start(f32[1,256,1,130]{1,3,2,0:T(8,128)} %get-tuple-element.329), channel_id=1, source_target_pairs={{0,4},{4,8},{8,12},{12,16},{16,20},{20,24},{24,28},{1,5},{5,9},{9,... | collective-permute-start | bytes 399368 | tf_op jit(solution)/shard_map/ppermute | solution.py:15
  64.8 1.5 select_bitcast_fusion.9
  66.4 2.7 rev.27
  69.0 2.8 collective-permute-done.2
  72.5 2.7 rev.26
  80.3 2.8 collective-permute-start.10
  83.2 2.1 copy-done.10
  86.4 1.5 scatter-add.105
  87.9 2.2 collective-permute-done.11
  91.0 1.5 scatter-add.106
  92.5 4.7 %multiply_convert_fusion = (bf16[1,256,8,128]{1,3,2,0:T(8,128)(2,1)S(1)}, bf16[1,256,8,128]{1,3,2,0:T(8,128)(2,1)S(1)}) fusion(f32[1,256,8,128]{1,3,2,0:T(8,128)} %scatter-add.106, bf16[9,256,256]{2,1,0:T(8,128)(2,1)} %param.58, bf16[1,9,256,8,128]{2,4,1,3,0:T(8,128)(2,1)} %copy-done.10), kind=kOutput, calls=%fused_computation.55 | convolution fusion | flops 1210843136 | bytes 7995392 | tf_op jit(solution)/shard_map/toc,btchw->bohw/dot_general | solution.py:65
  99.8 1.7 collective-permute-done.5
  101.5 2.3 collective-permute-start.7
  103.8 2.9 fusion.8
  107.8 5.6 %collective-permute-done.6 = bf16[1,256,1,130]{1,3,2,0:T(8,128)(2,1)S(1)} collective-permute-done((bf16[1,256,1,130]{1,3,2,0:T(8,128)(2,1)S(1)}, bf16[1,256,1,130]{1,3,2,0:T(8,128)(2,1)S(1)}, u32[]{:S(2)}, u32[]{:S(2)}) %collective-permute-start.6) | collective-permute-done | bytes 66592 | tf_op jit(solution)/shard_map/ppermute | solution.py:15
  115.1 2.1 copy-done.12
  117.2 2.9 fusion.11
  120.2 1.2 convolution_bitcast_fusion.8
  122.4 120.1 %all-reduce.7.cloned.1.call-done = (f32[9,256,256]{1,2,0:T(8,128)}, f32[9,256,256]{1,2,0:T(8,128)}) async-done(((f32[9,256,256]{1,2,0:T(8,128)}, f32[9,256,256]{1,2,0:T(8,128)}), (f32[9,256,256]{1,2,0:T(8,128)}, f32[9,256,256]{1,2,0:T(8,128)})) %all-reduce.7.cloned.1.call-update) | async-done | bytes 4718608 | tf_op jit(solution)/shard_map/psum | solution.py:119
  242.6 3.7 fusion.29
  246.3 7.0 %scatter-add.110 = f32[1,256,10,130]{1,3,2,0:T(8,128)S(1)} dynamic-update-slice(f32[1,256,10,130]{1,3,2,0:T(8,128)S(1)} %scatter-add.109, f32[1,256,8,128]{1,3,2,0:T(8,128)} %fusion.29, s32[]{:T(128)} %constant.657.clone.1, s32[]{:T(128)} %constant.657.clone.1, s32[]{:T(128)} %bitcast.51, s32[]{:T(128)} %bitcast.52) | dynamic-update-slice | bytes 2097156 | tf_op jit(solution)/shard_map/scatter-add | solution.py:81
  253.3 4.1 %add_select_fusion = f32[1,256,8,128]{1,3,2,0:T(8,128)} fusion(f32[1,256,10,130]{1,3,2,0:T(8,128)S(1)} %scatter-add.110, s32[]{:T(128)} %bitcast.57, s32[]{:T(128)} %bitcast.58, bf16[1,256,8,128]{1,3,2,0:T(8,128)(2,1)S(1)} %get-tuple-element.336, pred[]{:T(512)} %and_reduce_fusion, bf16[9,256,256]{2,1,0:T(8,128)(2,1)} %param.58), kind=kOutput, calls=%fused_computation.10 | convolution fusion | flops 134742016 | bytes 2754048 | tf_op jit(solution)/shard_map/oc,bohw->bchw/dot_general | solution.py:73
  257.4 7.2 %scatter-add.111 = f32[1,256,10,130]{1,3,2,0:T(8,128)S(1)} dynamic-update-slice(f32[1,256,10,130]{1,3,2,0:T(8,128)S(1)} %scatter-add.110, f32[1,256,8,128]{1,3,2,0:T(8,128)} %add_select_fusion, s32[]{:T(128)} %constant.657.clone.1, s32[]{:T(128)} %constant.657.clone.1, s32[]{:T(128)} %bitcast.57, s32[]{:T(128)} %bitcast.58) | dynamic-update-slice | bytes 2097156 | tf_op jit(solution)/shard_map/scatter-add | solution.py:81
  264.6 1.2 fusion.31
  265.8 2.2 fusion.32
  268.0 5.9 %scatter-add.115 = f32[1,256,10,130]{1,3,2,0:T(8,128)S(1)} dynamic-update-slice(f32[1,256,10,130]{1,3,2,0:T(8,128)S(1)} %fusion.31, f32[1,256,8,128]{1,3,2,0:T(8,128)} %fusion.32, s32[]{:T(128)} %constant.657.clone.1, s32[]{:T(128)} %constant.657.clone.1, s32[]{:T(128)} %constant.670.clone.1, s32[]{:T(128)} %constant.670.clone.1) | dynamic-update-slice | bytes 2097156 | tf_op jit(solution)/shard_map/scatter-add | solution.py:81
  273.8 2.2 fusion.33
  276.0 5.9 %scatter-add.116 = f32[1,256,10,130]{1,3,2,0:T(8,128)S(1)} dynamic-update-slice(f32[1,256,10,130]{1,3,2,0:T(8,128)S(1)} %scatter-add.115, f32[1,256,8,128]{1,3,2,0:T(8,128)} %fusion.33, s32[]{:T(128)} %constant.657.clone.1, s32[]{:T(128)} %constant.657.clone.1, s32[]{:T(128)} %constant.670.clone.1, s32[]{:T(128)} %constant.667.clone.1) | dynamic-update-slice | bytes 2097156 | tf_op jit(solution)/shard_map/scatter-add | solution.py:81
  281.9 1.2 fusion.35
  283.1 2.2 fusion.36
  285.3 5.9 %scatter-add.120 = f32[1,256,10,130]{1,3,2,0:T(8,128)S(1)} dynamic-update-slice(f32[1,256,10,130]{1,3,2,0:T(8,128)S(1)} %fusion.35, f32[1,256,8,128]{1,3,2,0:T(8,128)} %fusion.36, s32[]{:T(128)} %constant.657.clone.1, s32[]{:T(128)} %constant.657.clone.1, s32[]{:T(128)} %constant.667.clone.1, s32[]{:T(128)} %constant.670.clone.1) | dynamic-update-slice | bytes 2097156 | tf_op jit(solution)/shard_map/scatter-add | solution.py:81
  291.2 2.2 fusion.37
  293.3 5.9 %scatter-add.121 = f32[1,256,10,130]{1,3,2,0:T(8,128)S(1)} dynamic-update-slice(f32[1,256,10,130]{1,3,2,0:T(8,128)S(1)} %scatter-add.120, f32[1,256,8,128]{1,3,2,0:T(8,128)} %fusion.37, s32[]{:T(128)} %constant.657.clone.1, s32[]{:T(128)} %constant.657.clone.1, s32[]{:T(128)} %constant.667.clone.1, s32[]{:T(128)} %constant.667.clone.1) | dynamic-update-slice | bytes 2097156 | tf_op jit(solution)/shard_map/scatter-add | solution.py:81
  300.5 4.3 %collective-permute-start.12 = (f32[1,256,1,130]{1,3,2,0:T(8,128)}, f32[1,256,1,130]{1,3,2,0:T(8,128)S(1)}, u32[]{:S(2)}, u32[]{:S(2)}) collective-permute-start(f32[1,256,1,130]{1,3,2,0:T(8,128)} %get-tuple-element.325), channel_id=1, source_target_pairs={{0,4},{4,8},{8,12},{12,16},{16,20},{20,24},{24,28},{1,5},{5,9},{9,... | collective-permute-start | bytes 399368 | tf_op jit(solution)/shard_map/ppermute | solution.py:15
  305.2 1.4 collective-permute-start.13
  307.5 5.8 %collective-permute-done.13 = f32[1,256,1,130]{1,3,2,0:T(8,128)S(1)} collective-permute-done((f32[1,256,1,130]{1,3,2,0:T(8,128)S(1)}, f32[1,256,1,130]{1,3,2,0:T(8,128)S(1)}, u32[]{:S(2)}, u32[]{:S(2)}) %collective-permute-start.13) | collective-permute-done | bytes 133152 | tf_op jit(solution)/shard_map/ppermute | solution.py:17
  314.4 2.4 collective-permute-start.14
  316.8 4.0 %fusion.41 = bf16[1,256,8,128]{1,3,2,0:T(8,128)(2,1)S(1)} fusion(bf16[1,9,256,8,128]{2,4,3,1,0:T(8,128)(2,1)} %copy-done.12, bf16[9,256,256]{2,1,0:T(8,128)(2,1)S(1)} %copy-done.5, bf16[1,256,8,128]{1,3,2,0:T(8,128)(2,1)S(1)} %copy.9), kind=kOutput, calls=%fused_computation.51 | convolution fusion | flops 1208745984 | bytes 6946816 | tf_op jit(solution)/shard_map/toc,btchw->bohw/dot_general | solution.py:65
  320.8 1.1 copy.36
  322.2 4.3 %collective-permute-done.15 = f32[1,256,8,1]{1,3,2,0:T(1,128)S(1)} collective-permute-done((f32[1,256,8,1]{1,3,2,0:T(1,128)S(1)}, f32[1,256,8,1]{1,3,2,0:T(1,128)S(1)}, u32[]{:S(2)}, u32[]{:S(2)}) %collective-permute-start.15) | collective-permute-done | bytes 8224 | tf_op jit(solution)/shard_map/ppermute | solution.py:17
  327.8 35.3 %all-reduce.9.cloned.1.call-done = (f32[9,256,256]{1,2,0:T(8,128)}, f32[9,256,256]{1,2,0:T(8,128)}) async-done(((f32[9,256,256]{1,2,0:T(8,128)}, f32[9,256,256]{1,2,0:T(8,128)}), (f32[9,256,256]{1,2,0:T(8,128)}, f32[9,256,256]{1,2,0:T(8,128)})) %all-reduce.9.cloned.1.call-update) | async-done | bytes 4718608 | tf_op jit(solution)/shard_map/psum | solution.py:119
  363.1 3.2 copy.38
  366.3 1.9 copy.39
  (111 shorter events, 22.8 us)
Async XLA Ops:
  7.2 6.9 %copy-start = (bf16[1,256,8,128]{3,2,1,0:T(8,128)(2,1)S(1)}, bf16[1,256,8,128]{3,2,1,0:T(8,128)(2,1)}, u32[]{:S(2)}) copy-start(bf16[1,256,8,128]{3,2,1,0:T(8,128)(2,1)} %param.61) | copy-start | bytes 1572868
  7.2 235.4 %all-reduce.7.cloned.1.call-start = ((), (), s32[]{:S(2)}) async-start(), calls=%async_computation | async-start | bytes 9437184 | tf_op jit(solution)/shard_map/psum | solution.py:119
  8.6 42.0 %collective-permute-start = (bf16[1,256,8,1]{1,3,2,0:T(2,128)(2,1)S(1)}, bf16[1,256,8,1]{1,3,2,0:T(2,128)(2,1)S(1)}, u32[]{:S(2)}, u32[]{:S(2)}) collective-permute-start(bf16[1,256,8,1]{1,3,2,0:T(2,128)(2,1)S(1)} %get-tuple-element.348), channel_id=1, source_target_pairs={{0,32},{32,64},{64,96},{96,128},{128,160},{160,192},{192,224},{224... | collective-permute-start | bytes 12296 | tf_op jit(solution)/shard_map/ppermute | solution.py:15
  11.5 39.1 %collective-permute-start.1 = (bf16[1,256,8,1]{1,3,2,0:T(2,128)(2,1)S(1)}, bf16[1,256,8,1]{1,3,2,0:T(2,128)(2,1)S(1)}, u32[]{:S(2)}, u32[]{:S(2)}) collective-permute-start(bf16[1,256,8,1]{1,3,2,0:T(2,128)(2,1)S(1)} %get-tuple-element.349), channel_id=1, source_target_pairs={{32,0},{64,32},{96,64},{128,96},{160,128},{192,160},{224,192},{0,2... | collective-permute-start | bytes 12296 | tf_op jit(solution)/shard_map/ppermute | solution.py:17
  50.6 14.0 %copy-start.6 = (bf16[1,256,8,1]{1,3,2,0:T(2,128)(2,1)}, bf16[1,256,8,1]{1,3,2,0:T(2,128)(2,1)S(1)}, u32[]{:S(2)}) copy-start(bf16[1,256,8,1]{1,3,2,0:T(2,128)(2,1)S(1)} %collective-permute-done) | copy-start | bytes 12292
  50.6 14.0 %copy-start.8 = (bf16[1,256,8,1]{1,3,2,0:T(2,128)(2,1)}, bf16[1,256,8,1]{1,3,2,0:T(2,128)(2,1)S(1)}, u32[]{:S(2)}) copy-start(bf16[1,256,8,1]{1,3,2,0:T(2,128)(2,1)S(1)} %collective-permute-done.1) | copy-start | bytes 12292
  51.3 13.5 %collective-permute-start.3 = (bf16[1,256,1,130]{1,3,2,0:T(8,128)(2,1)}, bf16[1,256,1,130]{1,3,2,0:T(8,128)(2,1)}, u32[]{:S(2)}, u32[]{:S(2)}) collective-permute-start(bf16[1,256,1,130]{1,3,2,0:T(8,128)(2,1)} %get-tuple-element.344), channel_id=1, source_target_pairs={{4,0},{8,4},{12,8},{16,12},{20,16},{24,20},{28,24},{0,28},{5,1},{9... | collective-permute-start | bytes 199688 | tf_op jit(solution)/shard_map/ppermute | solution.py:17
  57.2 22.1 %collective-permute-start.9 = (f32[1,256,1,130]{1,3,2,0:T(8,128)}, f32[1,256,1,130]{1,3,2,0:T(8,128)}, u32[]{:S(2)}, u32[]{:S(2)}) collective-permute-start(f32[1,256,1,130]{1,3,2,0:T(8,128)} %get-tuple-element.328), channel_id=1, source_target_pairs={{4,0},{8,4},{12,8},{16,12},{20,16},{24,20},{28,24},{5,1},{9,5},{13... | collective-permute-start | bytes 399368 | tf_op jit(solution)/shard_map/ppermute | solution.py:17
  58.5 19.9 %collective-permute-start.8 = (f32[1,256,1,130]{1,3,2,0:T(8,128)}, f32[1,256,1,130]{1,3,2,0:T(8,128)}, u32[]{:S(2)}, u32[]{:S(2)}) collective-permute-start(f32[1,256,1,130]{1,3,2,0:T(8,128)} %get-tuple-element.329), channel_id=1, source_target_pairs={{0,4},{4,8},{8,12},{12,16},{16,20},{20,24},{24,28},{1,5},{5,9},{9,... | collective-permute-start | bytes 399368 | tf_op jit(solution)/shard_map/ppermute | solution.py:15
  64.7 7.2 %collective-permute-start.2 = (bf16[1,256,1,130]{1,3,2,0:T(8,128)(2,1)}, bf16[1,256,1,130]{1,3,2,0:T(8,128)(2,1)}, u32[]{:S(2)}, u32[]{:S(2)}) collective-permute-start(bf16[1,256,1,130]{1,3,2,0:T(8,128)(2,1)} %get-tuple-element.345), channel_id=1, source_target_pairs={{0,4},{4,8},{8,12},{12,16},{16,20},{20,24},{24,28},{28,0},{1,5},{5... | collective-permute-start | bytes 199688 | tf_op jit(solution)/shard_map/ppermute | solution.py:15
  77.2 0.7 copy-start.7
  77.3 0.7 copy-start.9
  80.3 6.1 %collective-permute-start.10 = (f32[1,256,8,1]{1,3,2,0:T(1,128)S(1)}, f32[1,256,8,1]{1,3,2,0:T(1,128)S(1)}, u32[]{:S(2)}, u32[]{:S(2)}) collective-permute-start(f32[1,256,8,1]{1,3,2,0:T(1,128)S(1)} %get-tuple-element.335), channel_id=1, source_target_pairs={{0,32},{32,64},{64,96},{96,128},{128,160},{160,192},{192,224},{224... | collective-permute-start | bytes 24584 | tf_op jit(solution)/shard_map/ppermute | solution.py:15
  83.2 2.2 copy-start.10
  86.4 3.7 collective-permute-start.11
  92.5 11.4 %copy-start.11 = (bf16[1,9,256,8,128]{2,4,1,3,0:T(8,128)(2,1)S(1)}, bf16[1,9,256,8,128]{2,4,1,3,0:T(8,128)(2,1)}, u32[]{:S(2)}) copy-start(bf16[1,9,256,8,128]{2,4,1,3,0:T(8,128)(2,1)} %copy-done.10) | copy-start | bytes 14155780
  97.2 2.6 collective-permute-start.4
  97.8 3.7 collective-permute-start.5
  101.5 5.9 %collective-permute-start.7 = (bf16[1,256,1,130]{1,3,2,0:T(8,128)(2,1)S(1)}, bf16[1,256,1,130]{1,3,2,0:T(8,128)(2,1)S(1)}, u32[]{:S(2)}, u32[]{:S(2)}) collective-permute-start(bf16[1,256,1,130]{1,3,2,0:T(8,128)(2,1)S(1)} %get-tuple-element.340), channel_id=1, source_target_pairs={{4,0},{8,4},{12,8},{16,12},{20,16},{24,20},{28,24},{0,28},{5,1},{9... | collective-permute-start | bytes 199688 | tf_op jit(solution)/shard_map/ppermute | solution.py:17
  106.7 6.8 %collective-permute-start.6 = (bf16[1,256,1,130]{1,3,2,0:T(8,128)(2,1)S(1)}, bf16[1,256,1,130]{1,3,2,0:T(8,128)(2,1)S(1)}, u32[]{:S(2)}, u32[]{:S(2)}) collective-permute-start(bf16[1,256,1,130]{1,3,2,0:T(8,128)(2,1)S(1)} %get-tuple-element.341), channel_id=1, source_target_pairs={{0,4},{4,8},{8,12},{12,16},{16,20},{20,24},{24,28},{28,0},{1,5},{5... | collective-permute-start | bytes 199688 | tf_op jit(solution)/shard_map/ppermute | solution.py:15
  115.0 2.2 copy-start.12
  120.1 243.0 %all-reduce.9.cloned.1.call-start = ((), (), s32[]{:S(2)}) async-start(), calls=%async_computation.1 | async-start | bytes 9437184 | tf_op jit(solution)/shard_map/psum | solution.py:119
  121.3 1.0 copy-start.1
  300.5 7.0 %collective-permute-start.12 = (f32[1,256,1,130]{1,3,2,0:T(8,128)}, f32[1,256,1,130]{1,3,2,0:T(8,128)S(1)}, u32[]{:S(2)}, u32[]{:S(2)}) collective-permute-start(f32[1,256,1,130]{1,3,2,0:T(8,128)} %get-tuple-element.325), channel_id=1, source_target_pairs={{0,4},{4,8},{8,12},{12,16},{16,20},{20,24},{24,28},{1,5},{5,9},{9,... | collective-permute-start | bytes 399368 | tf_op jit(solution)/shard_map/ppermute | solution.py:15
  305.2 11.7 %copy-start.5 = (bf16[9,256,256]{2,1,0:T(8,128)(2,1)S(1)}, bf16[9,256,256]{2,1,0:T(8,128)(2,1)}, u32[]{:S(2)}) copy-start(bf16[9,256,256]{2,1,0:T(8,128)(2,1)} %param.59) | copy-start | bytes 3538948
  305.2 8.1 %collective-permute-start.13 = (f32[1,256,1,130]{1,3,2,0:T(8,128)S(1)}, f32[1,256,1,130]{1,3,2,0:T(8,128)S(1)}, u32[]{:S(2)}, u32[]{:S(2)}) collective-permute-start(f32[1,256,1,130]{1,3,2,0:T(8,128)S(1)} %get-tuple-element.324), channel_id=1, source_target_pairs={{4,0},{8,4},{12,8},{16,12},{20,16},{24,20},{28,24},{5,1},{9,5},{13... | collective-permute-start | bytes 399368 | tf_op jit(solution)/shard_map/ppermute | solution.py:17
  313.4 1.0 copy-start.2
  314.4 7.7 %collective-permute-start.14 = (f32[1,256,8,1]{1,3,2,0:T(1,128)S(1)}, f32[1,256,8,1]{1,3,2,0:T(1,128)S(1)}, u32[]{:S(2)}, u32[]{:S(2)}) collective-permute-start(f32[1,256,8,1]{1,3,2,0:T(1,128)S(1)} %get-tuple-element.333), channel_id=1, source_target_pairs={{0,32},{32,64},{64,96},{96,128},{128,160},{160,192},{192,224},{224... | collective-permute-start | bytes 24584 | tf_op jit(solution)/shard_map/ppermute | solution.py:15
  316.8 5.1 %copy-start.3 = (f32[1,256,8,130]{1,3,2,0:T(8,128)S(1)}, f32[1,256,8,130]{1,3,2,0:T(8,128)}, u32[]{:S(2)}) copy-start(f32[1,256,8,130]{1,3,2,0:T(8,128)} %copy-done.2) | copy-start | bytes 3194884
  322.0 4.5 %collective-permute-start.15 = (f32[1,256,8,1]{1,3,2,0:T(1,128)S(1)}, f32[1,256,8,1]{1,3,2,0:T(1,128)S(1)}, u32[]{:S(2)}, u32[]{:S(2)}) collective-permute-start(f32[1,256,8,1]{1,3,2,0:T(1,128)S(1)} %get-tuple-element.332), channel_id=1, source_target_pairs={{32,0},{64,32},{96,64},{128,96},{160,128},{192,160},{224,192},{0,2... | collective-permute-start | bytes 24584 | tf_op jit(solution)/shard_map/ppermute | solution.py:17
  363.1 3.2 copy-start.4
Sparse Core Ops, SparseCore 0:
  120.2 122.2 all-reduce.6
  245.0 118.0 all-reduce.8
